TPU v7x, 512 devices: a whole 4x4x16 slice. The times are simulated.
512 devices in a mesh: inb: 16 (over y, z_lo), hid: 32 (over z_hi, x, core).
Axes of the slice: x: 4, y: 4, z: 16 (z_hi: 4, z_lo: 4; z = z_hi * 4 + z_lo), core: 2. Of those that a mesh axis runs over, the one named last changes fastest.
Arguments:
- activations: bfloat16 [2, 512, 16384], P(None, 'hid', 'inb'), may hold values from -40 to 40
- out_grads: bfloat16 [2, 512, 32768], P(None, 'inb', 'hid'), may hold values from -1 to 1
- basis_in: bfloat16 [16384, 1024], P('inb', 'hid'), may hold values from -0.1875 to 0.1875
- basis_out: bfloat16 [32768, 1024], P('hid', 'inb'), may hold values from -0.1875 to 0.1875
Outputs:
- precond: bfloat16 [16384, 32768], P('inb', 'hid')
All inputs are finite; a program needn't handle non-finite values.
Results may differ from a plain program's by a relative error of at most 0.0058.
Values may be sent and summed in bfloat16 or wider, within the bound.
A program may use at most 64 MiB of HBM per device.

v0:
```python
import jax
import jax.numpy as jnp
from jax import lax
from jax.sharding import PartitionSpec as P

damping = 0.1


def square_round(values):
    widened = values.astype(jnp.float32)
    return (widened * widened).astype(jnp.bfloat16)


def contract_tokens(left_side, right_side):
    return lax.dot_general(
        left_side, right_side, (((0, 1), (0, 1)), ((), ())), preferred_element_type=jnp.float32
    )


def on_device(activations, out_grads, basis_in, basis_out):
    micro_count = activations.shape[0]
    width_block = basis_in.shape[0]
    grads_flat = out_grads.reshape(-1, width_block)
    grads_rot = (
        jnp.dot(
            grads_flat,
            lax.all_gather(basis_out, "inb", axis=1, tiled=True),
            preferred_element_type=jnp.float32,
        )
        .astype(jnp.bfloat16)
        .reshape(out_grads.shape)
    )
    basis_whole = lax.all_gather(basis_in, "hid", axis=1, tiled=True)
    groups = [(number, number + 1) for number in range(micro_count)]
    grad_sum = jnp.zeros((width_block, width_block), jnp.float32)
    fisher_sum = jnp.zeros((width_block, width_block), jnp.float32)
    for lower_mb, upper_mb in groups:
        grads_full = lax.all_gather(grads_rot[lower_mb:upper_mb], "inb", axis=1, tiled=True)
        grads_squared = square_round(grads_full)
        plain_rows = lax.all_gather(activations[lower_mb:upper_mb], "hid", axis=1, tiled=True)
        rotated = (
            jnp.dot(
                plain_rows.reshape(-1, width_block), basis_whole, preferred_element_type=jnp.float32
            )
            .astype(jnp.bfloat16)
            .reshape(plain_rows.shape)
        )
        grad_sum = grad_sum + contract_tokens(rotated, grads_full)
        fisher_sum = fisher_sum + contract_tokens(square_round(rotated), grads_squared)
    return (grad_sum / (fisher_sum + damping)).astype(jnp.bfloat16)


def solution(mesh):
    return jax.shard_map(
        on_device,
        mesh=mesh,
        in_specs=(P(None, "hid", "inb"), P(None, "inb", "hid"), P("inb", "hid"), P("hid", "inb")),
        out_specs=P("inb", "hid"),
        check_vma=False,
    )
```

profile of v0, /device:TPU:2, one launch (start us, length us, event | category | flops | bytes accessed | tf_op | source)
XLA Modules:
  0.0 509.5 jit_solution(13084223138114623987)
XLA Ops:
  6.5 0.0 copy-start
  6.5 0.0 all-gather.13.cloned.1.call-start
  6.5 0.7 all-gather.13.cloned.1.call-update
  7.3 0.0 all-gather.15.cloned.1.call-start
  7.3 1.4 fusion.4
  8.7 0.0 all-gather.15.cloned.1.call-update
  8.7 0.0 all-gather.11.cloned.1.call-start
  8.8 0.7 all-gather.11.cloned.1.call-update
  9.5 0.0 all-gather.9.cloned.1.call-start
  9.5 0.5 all-gather.9.cloned.1.call-update
  10.0 0.0 all-gather.17.cloned.1.call-start
  10.1 95.8 %all-gather.13.cloned.1.call-done = bf16[1024,1024]{0,1:T(8,128)(2,1)} async-done(((bf16[1024,64]{0,1:T(8,128)(2,1)}), bf16[1024,1024]{0,1:T(8,128)(2,1)}) %all-gather.13.cloned.1.call-update) | async-done | bytes 2097168 | tf_op jit(solution)/shard_map/all_gather | solution.py:27
  105.8 0.0 copy-done
  105.8 2.3 convolution_convert_fusion.2
  108.2 0.7 fusion.3
  108.9 0.0 all-gather.17.cloned.1.call-update
  108.9 0.0 all-gather.19.cloned.1.call-start
  108.9 0.5 all-gather.19.cloned.1.call-update
  109.5 68.9 %all-gather.15.cloned.1.call-done = bf16[1,512,1024]{2,1,0:T(8,128)(2,1)} async-done(((bf16[1,16,1024]{2,1,0:T(8,128)(2,1)}), bf16[1,512,1024]{2,1,0:T(8,128)(2,1)}) %all-gather.15.cloned.1.call-update) | async-done | bytes 1048592 | tf_op jit(solution)/shard_map/all_gather | solution.py:40
  178.4 76.6 %all-gather.11.cloned.1.call-done = bf16[1024,1024]{0,1:T(8,128)(2,1)} async-done(((bf16[1024,32]{0,1:T(8,128)(2,1)}), bf16[1024,1024]{0,1:T(8,128)(2,1)}) %all-gather.11.cloned.1.call-update) | async-done | bytes 2097168 | tf_op jit(solution)/shard_map/all_gather | solution.py:33
  254.9 3.2 convolution_convert_fusion
  258.2 64.8 %all-gather.9.cloned.1.call-done = bf16[1,512,1024]{2,1,0:T(8,128)(2,1)} async-done(((bf16[1,16,1024]{2,1,0:T(8,128)(2,1)}), bf16[1,512,1024]{2,1,0:T(8,128)(2,1)}) %all-gather.9.cloned.1.call-update) | async-done | bytes 1048592 | tf_op jit(solution)/shard_map/all_gather | solution.py:40
  322.9 3.2 convolution_convert_fusion.1
  326.1 80.6 %all-gather.17.cloned.1.call-done = bf16[512,1024]{1,0:T(8,128)(2,1)} async-done(((bf16[32,1024]{1,0:T(8,128)(2,1)}), bf16[512,1024]{1,0:T(8,128)(2,1)}) %all-gather.17.cloned.1.call-update) | async-done | bytes 1048592 | tf_op jit(solution)/shard_map/all_gather | solution.py:38
  406.7 0.0 copy-start.2
  406.7 4.5 fusion
  411.2 0.0 copy-done.2
  411.2 3.3 fusion.5
  414.6 79.8 %all-gather.19.cloned.1.call-done = bf16[512,1024]{1,0:T(8,128)(2,1)} async-done(((bf16[32,1024]{1,0:T(8,128)(2,1)}), bf16[512,1024]{1,0:T(8,128)(2,1)}) %all-gather.19.cloned.1.call-update) | async-done | bytes 1048592 | tf_op jit(solution)/shard_map/all_gather | solution.py:38
  494.3 0.0 copy-start.1
  494.3 0.0 copy-start.3
  494.3 2.7 fusion.6
  497.0 0.0 copy-done.1
  497.0 0.1 copy-done.3
  497.1 5.5 %divide_convert_fusion = bf16[1024,1024]{1,0:T(8,128)(2,1)} fusion(f32[1024,1024]{1,0:T(8,128)} %fusion, f32[1024,1024]{1,0:T(8,128)S(1)} %copy-done.1, f32[1024,1024]{1,0:T(8,128)S(1)} %fusion.6, bf16[512,1024]{1,0:T(8,128)(2,1)S(1)} %convolution_convert_fusion, bf16[512,1024]{1,0:T(8,128)(2,1)S(1)} %copy-done.3), kind=kOutput, calls=%fused_computation | convolution fusion | flops 1082130432 | bytes 16777216 | tf_op jit(solution)/shard_map/dot_general | solution.py:15
Async XLA Ops:
  6.5 99.3 %copy-start = (bf16[2,32,1024]{2,1,0:T(8,128)(2,1)S(1)}, bf16[2,32,1024]{2,1,0:T(8,128)(2,1)}, u32[]{:S(2)}) copy-start(bf16[2,32,1024]{2,1,0:T(8,128)(2,1)} %param.5) | copy-start | bytes 393220
  6.5 99.3 %all-gather.13.cloned.1.call-start = ((), (), s32[]{:S(2)}) async-start(), calls=%async_computation.2 | async-start | bytes 2228224 | tf_op jit(solution)/shard_map/all_gather | solution.py:27
  7.3 171.1 %all-gather.15.cloned.1.call-start = ((), (), s32[]{:S(2)}) async-start(), calls=%async_computation.3 | async-start | bytes 1081344 | tf_op jit(solution)/shard_map/all_gather | solution.py:40
  8.7 246.2 %all-gather.11.cloned.1.call-start = ((), (), s32[]{:S(2)}) async-start(), calls=%async_computation.1 | async-start | bytes 2162688 | tf_op jit(solution)/shard_map/all_gather | solution.py:33
  9.5 313.4 %all-gather.9.cloned.1.call-start = ((), (), s32[]{:S(2)}) async-start(), calls=%async_computation | async-start | bytes 1081344 | tf_op jit(solution)/shard_map/all_gather | solution.py:40
  10.0 396.6 %all-gather.17.cloned.1.call-start = ((), (), s32[]{:S(2)}) async-start(), calls=%async_computation.4 | async-start | bytes 1114112 | tf_op jit(solution)/shard_map/all_gather | solution.py:38
  108.9 385.4 %all-gather.19.cloned.1.call-start = ((), (), s32[]{:S(2)}) async-start(), calls=%async_computation.5 | async-start | bytes 1114112 | tf_op jit(solution)/shard_map/all_gather | solution.py:38
  406.7 4.6 copy-start.2
  494.3 2.7 copy-start.1
  494.3 2.8 copy-start.3
Sparse Core Ops, SparseCore 0:
  9.4 96.3 all-gather.12
  109.0 69.3 all-gather.14
  181.5 73.3 all-gather.10
  257.9 64.9 all-gather.8
  324.8 81.8 all-gather.16
  408.6 85.6 all-gather.18
where the time goes:
time: 510 us; the launch traced here: 509 us
  waiting for transfers between devices  469 us (92%)
  matrix products  24.8 us (5%)
  between operations  13.5 us (3%)
    all_gather x2, waiting for transfers between devices, on_device(): lax.all_gather(grads_rot[lower_mb:upper_mb], 'inb', axis=1, tiled=True)  160 us
    all_gather x2, waiting for transfers between devices, on_device(): lax.all_gather(activations[lower_mb:upper_mb], 'hid', axis=1, tiled=True)  134 us
    all_gather x1, waiting for transfers between devices, on_device(): lax.all_gather(basis_out, 'inb', axis=1, tiled=True)  95.8 us
    all_gather x1, waiting for transfers between devices, on_device(): basis_whole = lax.all_gather(basis_in, 'hid', axis=1, tiled=True)  76.6 us
    dot_general x4, matrix products, contract_tokens(): lax.dot_general(left_side, right_side, (((0, 1), (0, 1)), ((), ())), pref...  16 us
  transfers between devices with their start and end apart: 6, of which 6 were waited for; matrix products, arithmetic and copies ran while one was open for 4% of the time, Pallas kernels for 0%

commit v1 on v0

--- a/solution.py
+++ b/solution.py
@@ -4,6 +4,11 @@
 from jax.sharding import PartitionSpec as P
 
 damping = 0.1
+
+
+def exchange_gather(value, axis, dim):
+    sent = jnp.stack([value] * lax.axis_size(axis))
+    return jnp.concatenate(lax.all_to_all(sent, axis, 0, 0), axis=dim)
 
 
 def square_round(values):
@@ -23,9 +28,7 @@
     grads_flat = out_grads.reshape(-1, width_block)
     grads_rot = (
         jnp.dot(
-            grads_flat,
-            lax.all_gather(basis_out, "inb", axis=1, tiled=True),
-            preferred_element_type=jnp.float32,
+            grads_flat, exchange_gather(basis_out, "inb", 1), preferred_element_type=jnp.float32
         )
         .astype(jnp.bfloat16)
         .reshape(out_grads.shape)

time: 510 us -> 431 us (0.85)
  the two profiles are of different devices: /device:TPU:2 before, /device:TPU:4 now
where the time goes in v1:
time: 431 us
  waiting for transfers between devices  381 us (88%)
  matrix products  23.2 us (5%)
  between operations  13.2 us (3%)
  starting transfers between devices  8.97 us (2%)
    all_gather x2, waiting for transfers between devices, on_device(): lax.all_gather(grads_rot[lower_mb:upper_mb], 'inb', axis=1, tiled=True)  161 us
    all_gather x2, waiting for transfers between devices, on_device(): lax.all_gather(activations[lower_mb:upper_mb], 'hid', axis=1, tiled=True)  91.4 us
    all_gather x1, waiting for transfers between devices, on_device(): basis_whole = lax.all_gather(basis_in, 'hid', axis=1, tiled=True)  77 us
    all_to_all x1, waiting for transfers between devices, exchange_gather(): return jnp.concatenate(lax.all_to_all(sent, axis, 0, 0), axis=dim)  50.1 us
    dot_general x4, matrix products, contract_tokens(): lax.dot_general(left_side, right_side, (((0, 1), (0, 1)), ((), ())), pref...  16 us
    all_to_all x1, starting transfers between devices, exchange_gather(): return jnp.concatenate(lax.all_to_all(sent, axis, 0, 0), axis=dim)  8.77 us
  transfers between devices with their start and end apart: 6, of which 6 were waited for; matrix products, arithmetic and copies ran while one was open for 4% of the time, Pallas kernels for 0%

profile of v1, /device:TPU:4, one launch (start us, length us, event | category | flops | bytes accessed | tf_op | source)
XLA Modules:
  0.0 430.5 jit_solution(1951010366498962563)
XLA Ops:
  6.5 0.0 copy-start
  6.5 2.5 stack.2
  9.1 0.0 copy-start.4
  9.1 8.8 %all-to-all-start = ((bf16[16,1024,64]{1,2,0:T(8,128)(2,1)}), bf16[16,1024,64]{1,2,0:T(8,128)(2,1)S(1)}, u32[]{:S(2)}, u32[]{:S(2)}) async-start(bf16[16,1024,64]{1,2,0:T(8,128)(2,1)} %stack.2), calls=%async_computation | async-start | bytes 4194304 | tf_op jit(solution)/shard_map/all_to_all | solution.py:11
  17.8 0.0 all-gather.12.cloned.1.call-start
  17.9 0.0 copy-done.4
  17.9 0.6 fusion.4
  18.5 0.0 all-gather.12.cloned.1.call-update
  18.6 0.0 all-gather.10.cloned.1.call-start
  18.6 0.7 all-gather.10.cloned.1.call-update
  19.3 0.0 all-gather.8.cloned.1.call-start
  19.4 0.7 all-gather.8.cloned.1.call-update
  20.1 0.0 all-gather.14.cloned.1.call-start
  20.1 50.1 %all-to-all-done = bf16[16,1024,64]{1,2,0:T(8,128)(2,1)S(1)} async-done(((bf16[16,1024,64]{1,2,0:T(8,128)(2,1)}), bf16[16,1024,64]{1,2,0:T(8,128)(2,1)S(1)}, u32[]{:S(2)}, u32[]{:S(2)}) %all-to-all-start) | async-done | bytes 2097184 | tf_op jit(solution)/shard_map/all_to_all | solution.py:11
  70.2 0.0 copy-done
  70.2 0.8 convolution_convert_fusion.2
  71.0 0.7 fusion.3
  71.6 0.0 all-gather.14.cloned.1.call-update
  71.6 0.0 all-gather.16.cloned.1.call-start
  71.7 0.5 all-gather.16.cloned.1.call-update
  72.2 26.9 %all-gather.12.cloned.1.call-done = bf16[1,512,1024]{2,1,0:T(8,128)(2,1)} async-done(((bf16[1,16,1024]{2,1,0:T(8,128)(2,1)}), bf16[1,512,1024]{2,1,0:T(8,128)(2,1)}) %all-gather.12.cloned.1.call-update) | async-done | bytes 1048592 | tf_op jit(solution)/shard_map/all_gather | solution.py:43
  99.1 77.0 %all-gather.10.cloned.1.call-done = bf16[1024,1024]{0,1:T(8,128)(2,1)} async-done(((bf16[1024,32]{0,1:T(8,128)(2,1)}), bf16[1024,1024]{0,1:T(8,128)(2,1)}) %all-gather.10.cloned.1.call-update) | async-done | bytes 2097168 | tf_op jit(solution)/shard_map/all_gather | solution.py:36
  176.1 3.2 convolution_convert_fusion
  179.3 64.5 %all-gather.8.cloned.1.call-done = bf16[1,512,1024]{2,1,0:T(8,128)(2,1)} async-done(((bf16[1,16,1024]{2,1,0:T(8,128)(2,1)}), bf16[1,512,1024]{2,1,0:T(8,128)(2,1)}) %all-gather.8.cloned.1.call-update) | async-done | bytes 1048592 | tf_op jit(solution)/shard_map/all_gather | solution.py:43
  243.8 3.2 convolution_convert_fusion.1
  247.0 80.9 %all-gather.14.cloned.1.call-done = bf16[512,1024]{1,0:T(8,128)(2,1)} async-done(((bf16[32,1024]{1,0:T(8,128)(2,1)}), bf16[512,1024]{1,0:T(8,128)(2,1)}) %all-gather.14.cloned.1.call-update) | async-done | bytes 1048592 | tf_op jit(solution)/shard_map/all_gather | solution.py:41
  327.8 0.0 copy-start.2
  327.8 4.6 %fusion.5 = f32[1024,1024]{1,0:T(8,128)} fusion(bf16[512,1024]{1,0:T(8,128)(2,1)S(1)} %convolution_convert_fusion.1, bf16[512,1024]{1,0:T(8,128)(2,1)} %all-gather.14.cloned.1.call-done), kind=kOutput, calls=%fused_computation.13 | convolution fusion | flops 1073741824 | bytes 6291456 | tf_op jit(solution)/shard_map/dot_general | solution.py:20
  332.4 0.0 copy-done.2
  332.5 3.2 fusion
  335.7 80.0 %all-gather.16.cloned.1.call-done = bf16[512,1024]{1,0:T(8,128)(2,1)} async-done(((bf16[32,1024]{1,0:T(8,128)(2,1)}), bf16[512,1024]{1,0:T(8,128)(2,1)}) %all-gather.16.cloned.1.call-update) | async-done | bytes 1048592 | tf_op jit(solution)/shard_map/all_gather | solution.py:41
  415.7 0.0 copy-start.1
  415.7 0.0 copy-start.3
  415.7 2.7 fusion.6
  418.3 0.0 copy-done.1
  418.3 0.1 copy-done.3
  418.5 5.5 %divide_convert_fusion = bf16[1024,1024]{1,0:T(8,128)(2,1)} fusion(f32[1024,1024]{1,0:T(8,128)} %fusion, f32[1024,1024]{1,0:T(8,128)S(1)} %copy-done.1, f32[1024,1024]{1,0:T(8,128)S(1)} %fusion.6, bf16[512,1024]{1,0:T(8,128)(2,1)S(1)} %convolution_convert_fusion, bf16[512,1024]{1,0:T(8,128)(2,1)S(1)} %copy-done.3), kind=kOutput, calls=%fused_computation | convolution fusion | flops 1082130432 | bytes 16777216 | tf_op jit(solution)/shard_map/dot_general | solution.py:20
Async XLA Ops:
  6.5 63.7 %copy-start = (bf16[2,32,1024]{2,1,0:T(8,128)(2,1)S(1)}, bf16[2,32,1024]{2,1,0:T(8,128)(2,1)}, u32[]{:S(2)}) copy-start(bf16[2,32,1024]{2,1,0:T(8,128)(2,1)} %param.5) | copy-start | bytes 393220
  9.1 8.8 %copy-start.4 = (bf16[2,16,1024]{2,1,0:T(8,128)(2,1)S(1)}, bf16[2,16,1024]{2,1,0:T(8,128)(2,1)}, u32[]{:S(2)}) copy-start(bf16[2,16,1024]{2,1,0:T(8,128)(2,1)} %param.4) | copy-start | bytes 196612
  9.1 61.1 %all-to-all-start = ((bf16[16,1024,64]{1,2,0:T(8,128)(2,1)}), bf16[16,1024,64]{1,2,0:T(8,128)(2,1)S(1)}, u32[]{:S(2)}, u32[]{:S(2)}) async-start(bf16[16,1024,64]{1,2,0:T(8,128)(2,1)} %stack.2), calls=%async_computation | async-start | bytes 4194304 | tf_op jit(solution)/shard_map/all_to_all | solution.py:11
  17.8 81.3 %all-gather.12.cloned.1.call-start = ((), (), s32[]{:S(2)}) async-start(), calls=%async_computation.3 | async-start | bytes 1081344 | tf_op jit(solution)/shard_map/all_gather | solution.py:43
  18.6 157.5 %all-gather.10.cloned.1.call-start = ((), (), s32[]{:S(2)}) async-start(), calls=%async_computation.2 | async-start | bytes 2162688 | tf_op jit(solution)/shard_map/all_gather | solution.py:36
  19.3 224.5 %all-gather.8.cloned.1.call-start = ((), (), s32[]{:S(2)}) async-start(), calls=%async_computation.1 | async-start | bytes 1081344 | tf_op jit(solution)/shard_map/all_gather | solution.py:43
  20.1 307.8 %all-gather.14.cloned.1.call-start = ((), (), s32[]{:S(2)}) async-start(), calls=%async_computation.4 | async-start | bytes 1114112 | tf_op jit(solution)/shard_map/all_gather | solution.py:41
  71.6 344.0 %all-gather.16.cloned.1.call-start = ((), (), s32[]{:S(2)}) async-start(), calls=%async_computation.5 | async-start | bytes 1114112 | tf_op jit(solution)/shard_map/all_gather | solution.py:41
  327.8 4.6 %copy-start.2 = (bf16[512,1024]{1,0:T(8,128)(2,1)S(1)}, bf16[512,1024]{1,0:T(8,128)(2,1)}, u32[]{:S(2)}) copy-start(bf16[512,1024]{1,0:T(8,128)(2,1)} %all-gather.14.cloned.1.call-done) | copy-start | bytes 3145732
  415.7 2.7 copy-start.1
  415.7 2.8 copy-start.3
Sparse Core Ops, SparseCore 0:
  21.8 77.2 all-gather.11
  102.2 73.8 all-gather.9
  179.2 64.4 all-gather.7
  245.7 82.0 all-gather.13
  329.8 85.8 all-gather.15
